TPU v7x, 512 devices: a whole 4x8x8 slice. The times are simulated.
512 devices in a mesh: items: 8 (over y), codes: 64 (over x, z, core).
Axes of the slice: x: 4, y: 8, z: 8, core: 2. Of those that a mesh axis runs over, the one named last changes fastest.
Arguments:
- residuals: bfloat16 [8192, 256], P(('items', 'codes')), may hold values from -6 to 6
- codebook: bfloat16 [16384, 256], P('codes'), may hold values from -6 to 6
Outputs:
- new_codebook: float32 [16384, 256], P('codes')
- next_residuals: float32 [8192, 256], P(('items', 'codes'))
All inputs are finite; a program needn't handle non-finite values.
Results may differ from a plain program's by a relative error of at most 0.0024.
Values may be sent and summed in bfloat16 or wider, within the bound.
No kernel may reach another device: no remote copies, remote signals or barrier semaphores. Data moves between devices by JAX's collectives and lax.ppermute only.
A program may use at most 64 MiB of HBM per device.

v0:
```python
import jax
import jax.numpy as jnp
from jax import lax
from jax.sharding import PartitionSpec as P

ITERS = 3
EPSILON = 1e-06
SHARPNESS = 40.0


def shards(residuals, codebook):
    gathered = lax.all_gather(residuals, "codes", axis=0, tiled=True)
    feature_count = gathered.shape[1]
    rows_float = gathered.astype(jnp.float32)
    codes_float = codebook.astype(jnp.float32)
    row_scale = lax.rsqrt(jnp.mean(rows_float * rows_float, axis=1) + EPSILON)
    code_scale = lax.rsqrt(jnp.mean(codes_float * codes_float, axis=1) + EPSILON)
    similarity = lax.dot_general(
        gathered, codebook, (((1,), (1,)), ((), ())), preferred_element_type=jnp.float32
    )
    kernel = jnp.exp(
        SHARPNESS * similarity * row_scale[:, None] * code_scale[None, :] / feature_count
    )
    balance = gathered.shape[0] * lax.axis_size("items") / codebook.shape[0]
    weights_rows = jnp.ones((gathered.shape[0],), jnp.float32)
    weights_cols = jnp.ones((codebook.shape[0],), jnp.float32)
    for sweep in range(ITERS):
        column_total = lax.psum(
            jnp.dot(weights_rows, kernel, precision=lax.Precision.HIGHEST), "items"
        )
        weights_cols = balance / column_total
        row_total = lax.psum(
            jnp.dot(kernel, weights_cols, precision=lax.Precision.HIGHEST), "codes"
        )
        weights_rows = 1.0 / row_total
    transport = (kernel * weights_rows[:, None] * weights_cols[None, :]).astype(jnp.bfloat16)
    numerator = lax.dot_general(
        transport, gathered, (((0,), (0,)), ((), ())), preferred_element_type=jnp.float32
    )
    mass = jnp.sum(transport.astype(jnp.float32), axis=0)
    numerator, mass = lax.psum((numerator, mass), "items")
    new_codebook = numerator / mass[:, None]
    moved = lax.all_to_all(transport, "codes", split_axis=0, concat_axis=1, tiled=True)
    rebuilt = jnp.dot(
        moved,
        lax.all_gather(codebook, "codes", axis=0, tiled=True),
        preferred_element_type=jnp.float32,
    )
    following = residuals.astype(jnp.float32) - rebuilt
    return (new_codebook, following)


def solution(mesh):
    return jax.shard_map(
        shards,
        mesh=mesh,
        in_specs=(P(("items", "codes"), None), P("codes", None)),
        out_specs=(P("codes", None), P(("items", "codes"), None)),
        check_vma=False,
    )
```

profile of v0, /device:TPU:1, one launch (start us, length us, event | category | flops | bytes accessed | tf_op | source)
XLA Modules:
  0.0 592.9 jit_solution(12532103684570617176)
XLA Ops:
  8.0 0.0 copy-start
  8.0 0.0 all-reduce.2.cloned.1.call-start
  8.1 57.9 %all_gather.6 = bf16[1024,256]{1,0:T(8,128)(2,1)S(1)} all-gather(bf16[16,256]{1,0:T(8,128)(2,1)} %param.2), channel_id=1, replica_groups=mesh['items'=8,'codes'=64] {'codes'}, dimensions={0}, use_global_device_ids=true | all-gather | bytes 532480 | tf_op jit(solution)/shard_map/all_gather | solution.py:12
  65.9 1.0 multiply_reduce_fusion.1
  67.0 0.2 multiply_reduce_fusion
  67.2 1.3 fusion.2
  68.5 0.5 fusion.3
  69.0 13.9 %psum.56 = f32[256]{0:T(256)S(1)} all-reduce(f32[256]{0:T(256)S(1)} %bitcast.44), channel_id=1, replica_groups=mesh['items'=8,'codes'=64] {'items'}, use_global_device_ids=true, to_apply=%region_2.0 | all-reduce | flops 256 | bytes 2048 | tf_op jit(solution)/shard_map/psum | solution.py:28
  82.9 1.0 fusion.6
  83.9 127.3 %psum.57 = f32[1024]{0:T(1024)S(1)} all-reduce(f32[1024]{0:T(1024)S(1)} %bitcast.34), channel_id=1, replica_groups=mesh['items'=8,'codes'=64] {'codes'}, use_global_device_ids=true, to_apply=%region_3.0 | all-reduce | flops 1024 | bytes 8192 | tf_op jit(solution)/shard_map/psum | solution.py:32
  211.2 0.5 fusion.7
  211.7 11.2 %psum.58 = f32[256]{0:T(256)S(1)} all-reduce(f32[256]{0:T(256)S(1)} %bitcast.41), channel_id=1, replica_groups=mesh['items'=8,'codes'=64] {'items'}, use_global_device_ids=true, to_apply=%region_4.0 | all-reduce | flops 256 | bytes 2048 | tf_op jit(solution)/shard_map/psum | solution.py:28
  222.9 1.0 fusion.8
  223.9 127.8 %psum.59 = f32[1024]{0:T(1024)S(1)} all-reduce(f32[1024]{0:T(1024)S(1)} %bitcast.36), channel_id=1, replica_groups=mesh['items'=8,'codes'=64] {'codes'}, use_global_device_ids=true, to_apply=%region_5.0 | all-reduce | flops 1024 | bytes 8192 | tf_op jit(solution)/shard_map/psum | solution.py:32
  351.7 0.5 fusion.9
  352.2 11.6 %psum.60 = f32[256]{0:T(256)S(1)} all-reduce(f32[256]{0:T(256)S(1)} %bitcast.43), channel_id=1, replica_groups=mesh['items'=8,'codes'=64] {'items'}, use_global_device_ids=true, to_apply=%region_6.0 | all-reduce | flops 256 | bytes 2048 | tf_op jit(solution)/shard_map/psum | solution.py:28
  363.8 1.0 fusion.10
  364.8 127.8 %psum.61 = f32[1024]{0:T(1024)S(1)} all-reduce(f32[1024]{0:T(1024)S(1)} %bitcast.38), channel_id=1, replica_groups=mesh['items'=8,'codes'=64] {'codes'}, use_global_device_ids=true, to_apply=%region_7.0 | all-reduce | flops 1024 | bytes 8192 | tf_op jit(solution)/shard_map/psum | solution.py:32
  492.6 1.1 convert_reduce_fusion
  493.7 2.1 fusion.11
  495.8 0.0 all-reduce.2.cloned.1.call-update
  495.8 0.0 all-gather.2.cloned.1.call-start
  495.8 0.5 all-gather.2.cloned.1.call-update
  496.4 4.7 all-to-all-start
  501.1 12.6 %psum.63 = f32[256]{0:T(256)S(1)} all-reduce(f32[256]{0:T(256)S(1)} %get-tuple-element.2), channel_id=1, replica_groups=mesh['items'=8,'codes'=64] {'items'}, use_global_device_ids=true, to_apply=%region_10.0 | all-reduce | flops 256 | bytes 2048 | tf_op jit(solution)/shard_map/psum | solution.py:41
  513.7 46.6 %all-reduce.2.cloned.1.call-done = f32[256,256]{1,0:T(8,128)} async-done(((f32[256,256]{1,0:T(8,128)}), f32[256,256]{1,0:T(8,128)}) %all-reduce.2.cloned.1.call-update) | async-done | bytes 262160 | tf_op jit(solution)/shard_map/psum | solution.py:41
  560.3 1.8 broadcast_divide_fusion
  562.1 0.0 all-to-all-done
  562.1 18.1 %all-gather.2.cloned.1.call-done = bf16[16384,256]{1,0:T(8,128)(2,1)} async-done(((bf16[256,256]{1,0:T(8,128)(2,1)}), bf16[16384,256]{1,0:T(8,128)(2,1)}) %all-gather.2.cloned.1.call-update) | async-done | bytes 8388624 | tf_op jit(solution)/shard_map/all_gather | solution.py:46
  580.2 0.0 copy-done
  580.2 5.2 convolution_subtract_fusion
  (9 shorter events, 0.1 us)
Async XLA Ops:
  8.0 572.3 %copy-start = (bf16[16,256]{1,0:T(8,128)(2,1)S(1)}, bf16[16,256]{1,0:T(8,128)(2,1)}, u32[]{:S(2)}) copy-start(bf16[16,256]{1,0:T(8,128)(2,1)} %param.2) | copy-start | bytes 24580
  8.0 552.3 %all-reduce.2.cloned.1.call-start = ((), (), s32[]{:S(2)}) async-start(), calls=%async_computation.1 | async-start | bytes 524288 | tf_op jit(solution)/shard_map/psum | solution.py:41
  495.8 84.5 %all-gather.2.cloned.1.call-start = ((), (), s32[]{:S(2)}) async-start(), calls=%async_computation.2 | async-start | bytes 8519680 | tf_op jit(solution)/shard_map/all_gather | solution.py:46
  496.4 65.7 %all-to-all-start = ((bf16[64,16,256]{2,1,0:T(8,128)(2,1)}), bf16[64,16,256]{2,1,0:T(8,128)(2,1)S(1)}, u32[]{:S(2)}, u32[]{:S(2)}) async-start(bf16[64,16,256]{2,1,0:T(8,128)(2,1)} %bitcast.11), calls=%async_computation | async-start | bytes 1048576 | tf_op jit(solution)/shard_map/all_to_all | solution.py:43
Sparse Core Ops, SparseCore 0:
  495.9 64.3 all-reduce.1
Sparse Core Ops, SparseCore 1:
  499.6 80.5 all-gather.1
where the time goes:
time: 593 us
  blocking collectives  490 us (83%)
  waiting for transfers between devices  65.2 us (11%)
  between operations  15.5 us (3%)
  matrix products  13 us (2%)
    psum x3, blocking collectives, shards(): lax.psum(jnp.dot(kernel, weights_cols, precision=lax.Precision.HIGHEST),...  383 us
    all_gather x1, blocking collectives, shards(): gathered = lax.all_gather(residuals, 'codes', axis=0, tiled=True)  57.9 us
    psum x1, waiting for transfers between devices, shards(): numerator, mass = lax.psum((numerator, mass), 'items')  46.6 us
    psum x3, blocking collectives, shards(): lax.psum(jnp.dot(weights_rows, kernel, precision=lax.Precision.HIGHEST),...  36.7 us
    all_gather x1, waiting for transfers between devices, shards(): lax.all_gather(codebook, 'codes', axis=0, tiled=True)  18.1 us
    psum x1, blocking collectives, shards(): numerator, mass = lax.psum((numerator, mass), 'items')  12.6 us
  transfers between devices with their start and end apart: 3, of which 2 were waited for; matrix products, arithmetic and copies ran while one was open for 0% of the time, Pallas kernels for 0%

commit v1 on v0

--- a/solution.py
+++ b/solution.py
@@ -9,7 +9,9 @@
 
 
 def shards(residuals, codebook):
-    gathered = lax.all_gather(residuals, "codes", axis=0, tiled=True)
+    gathered = jnp.concatenate(
+        lax.all_to_all(jnp.stack([residuals] * lax.axis_size("codes")), "codes", 0, 0), axis=0
+    )
     feature_count = gathered.shape[1]
     rows_float = gathered.astype(jnp.float32)
     codes_float = codebook.astype(jnp.float32)

time: 593 us -> 569 us (0.960)
  blocking collectives: 490 us -> 432 us
  waiting for transfers between devices: 65.2 us -> 81.6 us
  starting transfers between devices: 4.8 us -> 19.6 us
    all_gather x1 -> x0, blocking collectives: 57.9 us -> none  [shards(): gathered = lax.all_gather(residuals, 'codes', axis=0, tiled=True)]
    all_to_all x0 -> x1, waiting for transfers between devices: none -> 16.2 us  [shards(): lax.all_to_all(jnp.stack([residuals] * lax.axis_size('codes')), 'codes',...]
    all_to_all x0 -> x1, starting transfers between devices: none -> 14.8 us  [shards(): lax.all_to_all(jnp.stack([residuals] * lax.axis_size('codes')), 'codes',...]
  transfers between devices with their start and end apart: 3 -> 4, of which waited for: 2 -> 3; matrix products, arithmetic and copies ran while one was open for 0% -> 0% of each run, Pallas kernels for 0% -> 0%
where the time goes in v1:
time: 569 us; the launch traced here: 568 us
  blocking collectives  432 us (76%)
  waiting for transfers between devices  81.6 us (14%)
  starting transfers between devices  19.6 us (3%)
  between operations  15.5 us (3%)
  matrix products  13 us (2%)
    psum x3, blocking collectives, shards(): lax.psum(jnp.dot(kernel, weights_cols, precision=lax.Precision.HIGHEST),...  383 us
    psum x1, waiting for transfers between devices, shards(): numerator, mass = lax.psum((numerator, mass), 'items')  46.5 us
    psum x3, blocking collectives, shards(): lax.psum(jnp.dot(weights_rows, kernel, precision=lax.Precision.HIGHEST),...  36.7 us
    all_gather x1, waiting for transfers between devices, shards(): lax.all_gather(codebook, 'codes', axis=0, tiled=True)  18.4 us
    all_to_all x1, waiting for transfers between devices, shards(): lax.all_to_all(jnp.stack([residuals] * lax.axis_size('codes')), 'codes',...  16.2 us
    all_to_all x1, starting transfers between devices, shards(): lax.all_to_all(jnp.stack([residuals] * lax.axis_size('codes')), 'codes',...  14.8 us
    psum x1, blocking collectives, shards(): numerator, mass = lax.psum((numerator, mass), 'items')  12.6 us
  transfers between devices with their start and end apart: 4, of which 3 were waited for; matrix products, arithmetic and copies ran while one was open for 0% of the time, Pallas kernels for 0%

profile of v1, /device:TPU:1, one launch (start us, length us, event | category | flops | bytes accessed | tf_op | source)
XLA Modules:
  0.0 567.9 jit_solution(10860303087291857490)
XLA Ops:
  8.0 1.6 stack.2
  9.6 14.8 %all-to-all-start = ((bf16[64,16,256]{2,1,0:T(8,128)(2,1)}), bf16[64,16,256]{2,1,0:T(8,128)(2,1)S(1)}, u32[]{:S(2)}, u32[]{:S(2)}) async-start(bf16[64,16,256]{2,1,0:T(8,128)(2,1)} %stack.2), calls=%async_computation | async-start | bytes 1048576 | tf_op jit(solution)/shard_map/all_to_all | solution.py:13
  24.4 0.0 all-reduce.2.cloned.1.call-start
  24.5 1.0 multiply_reduce_fusion.1
  25.5 16.2 %all-to-all-done = bf16[64,16,256]{2,1,0:T(8,128)(2,1)S(1)} async-done(((bf16[64,16,256]{2,1,0:T(8,128)(2,1)}), bf16[64,16,256]{2,1,0:T(8,128)(2,1)S(1)}, u32[]{:S(2)}, u32[]{:S(2)}) %all-to-all-start) | async-done | bytes 524320 | tf_op jit(solution)/shard_map/all_to_all | solution.py:13
  41.7 0.2 multiply_reduce_fusion
  41.9 0.1 mul.50
  42.0 1.3 fusion.2
  43.3 0.5 fusion.3
  43.8 14.0 %psum.56 = f32[256]{0:T(256)S(1)} all-reduce(f32[256]{0:T(256)S(1)} %bitcast.47), channel_id=1, replica_groups=mesh['items'=8,'codes'=64] {'items'}, use_global_device_ids=true, to_apply=%region_2.0 | all-reduce | flops 256 | bytes 2048 | tf_op jit(solution)/shard_map/psum | solution.py:30
  57.8 1.0 fusion.6
  58.8 127.3 %psum.57 = f32[1024]{0:T(1024)S(1)} all-reduce(f32[1024]{0:T(1024)S(1)} %bitcast.37), channel_id=1, replica_groups=mesh['items'=8,'codes'=64] {'codes'}, use_global_device_ids=true, to_apply=%region_3.0 | all-reduce | flops 1024 | bytes 8192 | tf_op jit(solution)/shard_map/psum | solution.py:34
  186.1 0.5 fusion.7
  186.6 11.2 %psum.58 = f32[256]{0:T(256)S(1)} all-reduce(f32[256]{0:T(256)S(1)} %bitcast.44), channel_id=1, replica_groups=mesh['items'=8,'codes'=64] {'items'}, use_global_device_ids=true, to_apply=%region_4.0 | all-reduce | flops 256 | bytes 2048 | tf_op jit(solution)/shard_map/psum | solution.py:30
  197.8 1.0 fusion.8
  198.8 127.8 %psum.59 = f32[1024]{0:T(1024)S(1)} all-reduce(f32[1024]{0:T(1024)S(1)} %bitcast.39), channel_id=1, replica_groups=mesh['items'=8,'codes'=64] {'codes'}, use_global_device_ids=true, to_apply=%region_5.0 | all-reduce | flops 1024 | bytes 8192 | tf_op jit(solution)/shard_map/psum | solution.py:34
  326.6 0.5 fusion.9
  327.1 11.6 %psum.60 = f32[256]{0:T(256)S(1)} all-reduce(f32[256]{0:T(256)S(1)} %bitcast.46), channel_id=1, replica_groups=mesh['items'=8,'codes'=64] {'items'}, use_global_device_ids=true, to_apply=%region_6.0 | all-reduce | flops 256 | bytes 2048 | tf_op jit(solution)/shard_map/psum | solution.py:30
  338.7 1.0 fusion.10
  339.7 127.8 %psum.61 = f32[1024]{0:T(1024)S(1)} all-reduce(f32[1024]{0:T(1024)S(1)} %bitcast.41), channel_id=1, replica_groups=mesh['items'=8,'codes'=64] {'codes'}, use_global_device_ids=true, to_apply=%region_7.0 | all-reduce | flops 1024 | bytes 8192 | tf_op jit(solution)/shard_map/psum | solution.py:34
  467.5 1.1 convert_reduce_fusion
  468.6 2.1 fusion.11
  470.7 0.0 all-reduce.2.cloned.1.call-update
  470.7 0.0 all-gather.2.cloned.1.call-start
  470.7 0.5 all-gather.2.cloned.1.call-update
  471.3 4.7 all-to-all-start.1
  476.0 12.6 %psum.63 = f32[256]{0:T(256)S(1)} all-reduce(f32[256]{0:T(256)S(1)} %get-tuple-element.2), channel_id=1, replica_groups=mesh['items'=8,'codes'=64] {'items'}, use_global_device_ids=true, to_apply=%region_10.0 | all-reduce | flops 256 | bytes 2048 | tf_op jit(solution)/shard_map/psum | solution.py:43
  488.6 46.5 %all-reduce.2.cloned.1.call-done = f32[256,256]{1,0:T(8,128)} async-done(((f32[256,256]{1,0:T(8,128)}), f32[256,256]{1,0:T(8,128)}) %all-reduce.2.cloned.1.call-update) | async-done | bytes 262160 | tf_op jit(solution)/shard_map/psum | solution.py:43
  535.1 1.8 broadcast_divide_fusion
  536.9 0.0 all-to-all-done.1
  536.9 18.4 %all-gather.2.cloned.1.call-done = bf16[16384,256]{1,0:T(8,128)(2,1)} async-done(((bf16[256,256]{1,0:T(8,128)(2,1)}), bf16[16384,256]{1,0:T(8,128)(2,1)}) %all-gather.2.cloned.1.call-update) | async-done | bytes 8388624 | tf_op jit(solution)/shard_map/all_gather | solution.py:48
  555.3 5.2 convolution_subtract_fusion
  (11 shorter events, 0.1 us)
Async XLA Ops:
  8.0 547.3 %copy-start = (bf16[16,256]{1,0:T(8,128)(2,1)S(1)}, bf16[16,256]{1,0:T(8,128)(2,1)}, u32[]{:S(2)}) copy-start(bf16[16,256]{1,0:T(8,128)(2,1)} %param.2) | copy-start | bytes 24580
  9.6 32.1 %all-to-all-start = ((bf16[64,16,256]{2,1,0:T(8,128)(2,1)}), bf16[64,16,256]{2,1,0:T(8,128)(2,1)S(1)}, u32[]{:S(2)}, u32[]{:S(2)}) async-start(bf16[64,16,256]{2,1,0:T(8,128)(2,1)} %stack.2), calls=%async_computation | async-start | bytes 1048576 | tf_op jit(solution)/shard_map/all_to_all | solution.py:13
  24.4 510.7 %all-reduce.2.cloned.1.call-start = ((), (), s32[]{:S(2)}) async-start(), calls=%async_computation.2 | async-start | bytes 524288 | tf_op jit(solution)/shard_map/psum | solution.py:43
  470.7 84.6 %all-gather.2.cloned.1.call-start = ((), (), s32[]{:S(2)}) async-start(), calls=%async_computation.3 | async-start | bytes 8519680 | tf_op jit(solution)/shard_map/all_gather | solution.py:48
  471.3 65.6 %all-to-all-start.1 = ((bf16[64,16,256]{2,1,0:T(8,128)(2,1)}), bf16[64,16,256]{2,1,0:T(8,128)(2,1)S(1)}, u32[]{:S(2)}, u32[]{:S(2)}) async-start(bf16[64,16,256]{2,1,0:T(8,128)(2,1)} %bitcast.12), calls=%async_computation.1 | async-start | bytes 1048576 | tf_op jit(solution)/shard_map/all_to_all | solution.py:45
Sparse Core Ops, SparseCore 0:
  470.8 64.2 all-reduce.1
Sparse Core Ops, SparseCore 1:
  474.5 80.7 all-gather.1
